TPU v7x, 32 devices: a whole 2x2x4 slice. The times are simulated.
32 devices in a mesh: comp: 2 (over core), gx: 4 (over y, x), gy: 4 (over z).
Axes of the slice: x: 2, y: 2, z: 4, core: 2. Of those that a mesh axis runs over, the one named last changes fastest.
Arguments:
- state: float32 [2, 8, 96, 3072], P('comp', None, 'gx', 'gy'), may hold values from -6 to 6
- response: float32 [2, 8, 3072], P('comp'), may hold values from -0.95 to 0
- diffusion: float32 [2, 96, 3072], P('comp', 'gx', 'gy'), may hold values from 0.02 to 0.24
- land_mask: int32 [96, 3072], P('gx', 'gy'), may hold values 0 or 1
- couple_src: int32 [2, 4, 4, 16, 128], P('comp', 'gx', 'gy'), may hold values from 0 to 18431
- couple_dst: int32 [2, 4, 4, 16, 128], P('comp', 'gx', 'gy'), may hold values from 0 to 18431
- couple_weight: float32 [2, 4, 4, 16, 128], P('comp', 'gx', 'gy'), may hold values from 0.1 to 1
- couple_count: int32 [2, 4, 4, 16], P('comp', 'gx', 'gy'), may hold values from 0 to 128, as said below
Outputs:
- final_state: float32 [2, 8, 96, 3072], P('comp', None, 'gx', 'gy')
Inputs may be any that keep to these rules, and one draw needn't show every extreme that they name: `couple_count`: at most 128 live slots per ordered device pair; every sending device has one pair with exactly 128.
All inputs are finite; a program needn't handle non-finite values. No bound on the sum of `land_mask` on one device may be relied on, other than what follows from the above.
Results may differ from a plain program's by a relative error of at most 0.0095.
Values may be sent and summed in bfloat16 or wider, within the bound.
A program may use at most 128 MiB of HBM per device.

v0:
```python
import math
import jax
import jax.numpy as jnp
from jax import lax
from jax.sharding import PartitionSpec as P

FC = 4


def extended(block, sides, width):
    for axis, dim in sides:
        count = lax.axis_size(axis)
        forward = [(i, i + 1) for i in range(count - 1)]
        backward = [(target, source) for source, target in forward]
        low = lax.ppermute(
            lax.slice_in_dim(block, block.shape[dim] - width, None, axis=dim), axis, forward
        )
        high = lax.ppermute(lax.slice_in_dim(block, 0, width, axis=dim), axis, backward)
        block = jnp.concatenate([low, block, high], axis=dim)
    return block


def partner(value, axis, stride):
    mask = 2**stride
    pairs = [(source, source ^ mask) for source in range(lax.axis_size(axis))]
    return lax.ppermute(value, axis, pairs)


def make_table(cols):
    rows_idx = jnp.arange(cols, dtype=jnp.int32)[:, None]
    wave_idx = jnp.arange(cols // 2, dtype=jnp.int32)[None, :]
    phase = rows_idx * wave_idx % cols
    angle = phase.astype(jnp.float32) * (2.0 * math.pi / cols)
    return jnp.concatenate([jnp.cos(angle), jnp.sin(angle)], axis=1).astype(jnp.bfloat16)


def back_transform(filtered, table_part):
    return lax.dot_general(
        filtered, table_part, (((1,), (1,)), ((), ())), preferred_element_type=jnp.float32
    )


def circle_increment(circles, resp_part, table, scale):
    count, rows_part, cols_all = circles.shape
    spec = jnp.dot(circles.reshape(-1, cols_all), table, preferred_element_type=jnp.float32)
    spec = spec.reshape(count, rows_part, cols_all)
    filtered = (spec * resp_part[:, None, :]).astype(jnp.bfloat16)
    incr = (back_transform(filtered.reshape(-1, cols_all), table) * scale).astype(jnp.bfloat16)
    return incr.reshape(count, rows_part, cols_all)


def diffuse(fields, rate):
    padded = extended(fields.astype(jnp.bfloat16), (("gx", 1),), 1).astype(fields.dtype)
    return fields + rate[None] * (padded[:, 2:] + padded[:, :-2] - 2.0 * fields)


def local(
    state, response, diffusion, land_mask, couple_src, couple_dst, couple_weight, couple_count
):
    levels, rows_dev, cols_dev = (state.shape[1], state.shape[2], state.shape[3])
    groups_x = lax.axis_size("gx")
    groups_y = lax.axis_size("gy")
    peers = groups_x * groups_y
    slots = couple_src.shape[4]
    cells = rows_dev * cols_dev
    cols_all = cols_dev * groups_y
    per_level = levels // groups_y
    section = lax.axis_index("comp")
    keep = jnp.where(section == 1, land_mask.astype(jnp.float32), jnp.float32(1.0))
    table = make_table(cols_all)
    scale = 2.0 / cols_all
    src_idx = couple_src.reshape(peers, slots)
    dst_idx = couple_dst.reshape(peers, slots)
    live = jnp.arange(slots, dtype=jnp.int32)[None, :] < couple_count.reshape(peers, 1)
    weights = jnp.where(live, couple_weight.reshape(peers, slots), jnp.float32(0.0))
    first_level = lax.axis_index("gy") * per_level
    resp_mine = lax.dynamic_slice_in_dim(response[0], first_level, per_level, 0)
    rate = diffusion[0]
    fields = state[0]
    surface = fields[:FC].reshape(FC, cells)
    outgoing = jnp.transpose(surface[:, src_idx] * weights[None], (1, 0, 2))
    crossed = partner(outgoing, "comp", 0)
    arrived = lax.all_to_all(crossed, ("gx", "gy"), split_axis=0, concat_axis=0, tiled=True)
    incoming = jnp.transpose(arrived, (1, 0, 2))
    surface = surface.at[:, dst_idx].add(incoming)
    surf = surface.reshape(FC, rows_dev, cols_dev)
    fields = jnp.concatenate([surf, fields[FC:]], axis=0)
    grid_bf = fields.astype(jnp.bfloat16)
    circles = lax.all_to_all(grid_bf, "gy", split_axis=0, concat_axis=2, tiled=True)
    incr = circle_increment(circles, resp_mine, table, scale)
    incr = lax.all_to_all(incr, "gy", split_axis=2, concat_axis=0, tiled=True)
    fields = fields + incr.astype(jnp.float32)
    fields = diffuse(fields, rate) * keep[None]
    return fields[None]


def solution(mesh):
    return jax.shard_map(
        local,
        mesh=mesh,
        in_specs=(
            P("comp", None, "gx", "gy"),
            P("comp", None, None),
            P("comp", "gx", "gy"),
            P("gx", "gy"),
            P("comp", "gx", "gy", None, None),
            P("comp", "gx", "gy", None, None),
            P("comp", "gx", "gy", None, None),
            P("comp", "gx", "gy", None),
        ),
        out_specs=P("comp", None, "gx", "gy"),
        check_vma=False,
    )
```

profile of v0, /device:TPU:4, one launch (start us, length us, event | category | flops | bytes accessed | tf_op | source)
XLA Modules:
  0.0 198.0 jit_solution(5701691548152781341)
XLA Ops:
  0.0 0.0 copy-start
  0.0 0.0 copy-start.2
  0.0 0.0 copy-start.3
  0.0 0.0 copy-start.5
  0.0 0.0 copy-start.4
  0.0 1.1 fusion.28
  1.2 0.0 copy-start.1
  1.2 5.6 %copy.20 = f32[1,4,24,768]{1,3,2,0:T(8,128)} copy(f32[1,4,24,768]{3,2,1,0:T(8,128)S(1)} %get-tuple-element.5) | data formatting | bytes 589824 | tf_op jit(solution)/shard_map/slice | solution.py:80
  6.8 0.0 copy-done.2
  6.8 9.1 %gather_fusion = f32[2048,4]{1,0:T(8,128)S(1)} fusion(f32[4,18432]{0,1:T(8,128)} %bitcast.55, s32[2048]{0:T(1024)S(1)} %fusion.25), kind=kCustom, calls=%fused_computation | custom fusion | bytes 73728 | tf_op jit(solution)/shard_map/gather | solution.py:81
  16.0 0.3 copy.21
  16.3 0.0 copy-done.3
  16.3 0.0 copy-done.5
  16.3 0.1 bitcast_select_fusion
  16.4 0.1 collective-permute-start
  16.5 1.2 collective-permute-done
  17.7 0.6 copy.22
  18.3 7.3 %all-to-all-start = ((f32[16,4,128]{2,1,0:T(4,128)}), f32[16,4,128]{2,1,0:T(4,128)S(1)}, u32[]{:S(2)}, u32[]{:S(2)}) async-start(f32[16,4,128]{2,1,0:T(4,128)} %copy.22), calls=%async_computation | async-start | bytes 65536 | tf_op jit(solution)/shard_map/all_to_all | solution.py:83
  25.6 0.0 copy-done.4
  25.6 6.1 %all-to-all-done = f32[16,4,128]{2,1,0:T(4,128)S(1)} async-done(((f32[16,4,128]{2,1,0:T(4,128)}), f32[16,4,128]{2,1,0:T(4,128)S(1)}, u32[]{:S(2)}, u32[]{:S(2)}) %all-to-all-start) | async-done | bytes 32800 | tf_op jit(solution)/shard_map/all_to_all | solution.py:83
  31.7 0.4 copy.23
  32.0 17.6 %scatter_fusion = f32[4,18432]{0,1:T(8,128)} fusion(f32[4,18432]{0,1:T(8,128)} %bitcast.56, s32[2048]{0:T(1024)S(1)} %fusion.23, f32[2048,4]{1,0:T(8,128)S(1)} %copy.23), kind=kCustom, calls=%fused_computation.1 | custom fusion | flops 8192 | bytes 106496 | tf_op jit(solution)/shard_map/scatter-add | solution.py:85
  49.7 6.4 %copy.24 = f32[4,24,768]{2,1,0:T(8,128)S(1)} copy(f32[4,24,768]{0,2,1:T(8,128)} %bitcast.57) | data formatting | bytes 589824 | tf_op jit(solution)/shard_map/reshape | solution.py:86
  56.1 0.0 copy-done.1
  56.1 0.7 fusion.21
  56.8 3.5 %all-to-all-start.1 = ((bf16[8,24,768]{2,1,0:T(8,128)(2,1)}), bf16[8,24,768]{2,1,0:T(8,128)(2,1)S(1)}, u32[]{:S(2)}, u32[]{:S(2)}) async-start(bf16[8,24,768]{2,1,0:T(8,128)(2,1)} %fusion.21), calls=%async_computation.1 | async-start | bytes 589824 | tf_op jit(solution)/shard_map/all_to_all | solution.py:89
  60.3 79.5 %sine_convert_fusion = (bf16[3072,1536]{1,0:T(8,128)(2,1)}, bf16[3072,1536]{1,0:T(8,128)(2,1)}) fusion(), kind=kLoop, calls=%fused_computation.8 | loop fusion | flops 51904512 | bytes 18874368 | tf_op jit(solution)/shard_map/convert.4
  139.8 0.0 copy-done
  139.8 0.0 all-to-all-done.1
  139.8 0.2 copy.29
  140.0 0.2 dot_general.8
  140.2 8.2 %fusion.12 = bf16[2,24,3072]{2,1,0:T(8,128)(2,1)S(1)} fusion(bf16[2,24,3072]{2,1,0:T(8,128)(2,1)S(1)} %dot_general.8, bf16[3072,1536]{1,0:T(8,128)(2,1)} %get-tuple-element.9, bf16[3072,1536]{1,0:T(8,128)(2,1)} %get-tuple-element.10, f32[2,3072]{1,0:T(2,128)S(1)} %dynamic-slice_bitcast_fusion), kind=kOutput, calls=%fused_computation.17 | convolution fusion | flops 944013312 | bytes 19488768 | tf_op jit(solution)/shard_map/dot_general | solution.py:45
  148.4 9.6 %fusion.15 = bf16[48,3072]{1,0:T(8,128)(2,1)S(1)} fusion(bf16[48,3072]{1,0:T(8,128)(2,1)S(1)} %bitcast.67, bf16[3072,1536]{1,0:T(8,128)(2,1)} %get-tuple-element.9, bf16[3072,1536]{1,0:T(8,128)(2,1)} %get-tuple-element.10), kind=kOutput, calls=%fused_computation.18 | convolution fusion | flops 944013312 | bytes 19464192 | tf_op jit(solution)/shard_map/dot_general | solution.py:38
  158.1 1.9 copy.26
  160.0 2.6 %reshape.148 = bf16[4,2,18432]{2,1,0:T(2,128)(2,1)} reshape(bf16[3072,2,24]{2,1,0:T(2,128)(2,1)S(1)} %bitcast.58) | data formatting | bytes 589824
  162.6 5.0 %all-to-all-start.2 = ((bf16[4,2,18432]{2,1,0:T(2,128)(2,1)}), bf16[4,2,18432]{2,1,0:T(2,128)(2,1)S(1)}, u32[]{:S(2)}, u32[]{:S(2)}) async-start(bf16[4,2,18432]{2,1,0:T(2,128)(2,1)} %reshape.148), calls=%async_computation.2 | async-start | bytes 589824 | tf_op jit(solution)/shard_map/all_to_all | solution.py:91
  167.7 8.3 %all-to-all-done.2 = bf16[4,2,18432]{2,1,0:T(2,128)(2,1)S(1)} async-done(((bf16[4,2,18432]{2,1,0:T(2,128)(2,1)}), bf16[4,2,18432]{2,1,0:T(2,128)(2,1)S(1)}, u32[]{:S(2)}, u32[]{:S(2)}) %all-to-all-start.2) | async-done | bytes 294944 | tf_op jit(solution)/shard_map/all_to_all | solution.py:91
  176.0 3.1 %reshape.149 = bf16[3072,2,24]{2,1,0:T(2,128)(2,1)} reshape(bf16[4,2,18432]{2,1,0:T(2,128)(2,1)S(1)} %all-to-all-done.2) | data formatting | bytes 589824
  179.1 2.5 %convert_bitcast_fusion = f32[4,2,24,768]{2,1,3,0:T(2,128)S(1)} fusion(bf16[2,24,4,768]{1,0,3,2:T(2,128)(2,1)} %bitcast.59), kind=kLoop, calls=%fused_computation.19 | loop fusion | flops 147456 | bytes 884736 | tf_op jit(solution)/shard_map/convert_element_type | solution.py:92
  181.6 2.8 %copy.27 = f32[4,2,24,768]{3,2,1,0:T(8,128)} copy(f32[4,2,24,768]{2,1,3,0:T(2,128)S(1)} %convert_bitcast_fusion) | data formatting | bytes 1179648 | tf_op jit(solution)/shard_map/convert_element_type | solution.py:92
  184.4 1.2 fusion.22
  185.7 3.4 %collective-permute-start.2 = (bf16[8,1,768]{2,1,0:T(2,128)(2,1)S(1)}, bf16[8,1,768]{2,1,0:T(2,128)(2,1)S(1)}, u32[]{:S(2)}, u32[]{:S(2)}) collective-permute-start(bf16[8,1,768]{2,1,0:T(2,128)(2,1)S(1)} %get-tuple-element.8), channel_id=1, source_target_pairs={{4,0},{8,4},{12,8},{5,1},{9,5},{13,9},{6,2},{10,6},{14,10},{7,3},{... | collective-permute-start | bytes 36872 | tf_op jit(solution)/shard_map/ppermute | solution.py:18
  189.0 2.5 %collective-permute-start.1 = (bf16[8,1,768]{2,1,0:T(2,128)(2,1)S(1)}, bf16[8,1,768]{2,1,0:T(2,128)(2,1)S(1)}, u32[]{:S(2)}, u32[]{:S(2)}) collective-permute-start(bf16[8,1,768]{2,1,0:T(2,128)(2,1)S(1)} %get-tuple-element.7), channel_id=1, source_target_pairs={{0,4},{4,8},{8,12},{1,5},{5,9},{9,13},{2,6},{6,10},{10,14},{3,7},{... | collective-permute-start | bytes 36872 | tf_op jit(solution)/shard_map/ppermute | solution.py:15
  191.5 0.9 convert_select_fusion
  192.4 0.0 collective-permute-done.2
  192.4 3.2 %collective-permute-done.1 = bf16[8,1,768]{2,1,0:T(2,128)(2,1)S(1)} collective-permute-done((bf16[8,1,768]{2,1,0:T(2,128)(2,1)S(1)}, bf16[8,1,768]{2,1,0:T(2,128)(2,1)S(1)}, u32[]{:S(2)}, u32[]{:S(2)}) %collective-permute-start.1) | collective-permute-done | bytes 12320 | tf_op jit(solution)/shard_map/ppermute | solution.py:15
  195.7 0.1 maximum_convert_fusion
  195.8 2.2 %fusion.20 = f32[1,8,24,768]{3,2,1,0:T(8,128)} fusion(f32[8,26,768]{2,1,0:T(8,128)S(1)} %maximum_convert_fusion, f32[24,768]{1,0:T(8,128)S(1)} %convert_select_fusion, f32[24,768]{1,0:T(8,128)} %bitcast.65, f32[4,2,24,768]{3,2,1,0:T(8,128)} %copy.27, f32[4,24,768]{2,1,0:T(8,128)} %copy-done.1, f32[4,24,768]{2,1,0:T(8,128)S(1)} %copy.24), kind=kLoop, calls=%fused_computation.25 | loop fusion | flops 1179648 | bytes 3096576 | tf_op jit(solution)/shard_map/broadcast_in_dim | solution.py:94
  (5 shorter events, 0.1 us)
Async XLA Ops:
  0.0 139.8 %copy-start = (f32[1,8,3072]{2,1,0:T(8,128)S(1)}, f32[1,8,3072]{2,1,0:T(8,128)}, u32[]{:S(2)}) copy-start(f32[1,8,3072]{2,1,0:T(8,128)} %param.9) | copy-start | bytes 294916
  0.0 6.8 %copy-start.2 = (s32[1,1,1,16,128]{4,3,2,1,0:T(8,128)S(1)}, s32[1,1,1,16,128]{4,3,2,1,0:T(8,128)}, u32[]{:S(2)}) copy-start(s32[1,1,1,16,128]{4,3,2,1,0:T(8,128)} %param.12) | copy-start | bytes 24580
  0.0 16.3 %copy-start.3 = (f32[1,1,1,16,128]{4,3,2,1,0:T(8,128)S(1)}, f32[1,1,1,16,128]{4,3,2,1,0:T(8,128)}, u32[]{:S(2)}) copy-start(f32[1,1,1,16,128]{4,3,2,1,0:T(8,128)} %param.14) | copy-start | bytes 24580
  0.0 16.3 %copy-start.5 = (s32[1,1,1,16]{3,2,1,0:T(1,128)S(1)}, s32[1,1,1,16]{3,2,1,0:T(1,128)}, u32[]{:S(2)}) copy-start(s32[1,1,1,16]{3,2,1,0:T(1,128)} %param.15) | copy-start | bytes 196
  0.0 25.6 %copy-start.4 = (s32[1,1,1,16,128]{4,3,2,1,0:T(8,128)S(1)}, s32[1,1,1,16,128]{4,3,2,1,0:T(8,128)}, u32[]{:S(2)}) copy-start(s32[1,1,1,16,128]{4,3,2,1,0:T(8,128)} %param.13) | copy-start | bytes 24580
  1.2 54.9 %copy-start.1 = (f32[4,24,768]{2,1,0:T(8,128)}, f32[4,24,768]{2,1,0:T(8,128)S(1)}, u32[]{:S(2)}) copy-start(f32[4,24,768]{2,1,0:T(8,128)S(1)} %get-tuple-element.6) | copy-start | bytes 884740
  16.4 1.3 collective-permute-start
  18.3 13.4 %all-to-all-start = ((f32[16,4,128]{2,1,0:T(4,128)}), f32[16,4,128]{2,1,0:T(4,128)S(1)}, u32[]{:S(2)}, u32[]{:S(2)}) async-start(f32[16,4,128]{2,1,0:T(4,128)} %copy.22), calls=%async_computation | async-start | bytes 65536 | tf_op jit(solution)/shard_map/all_to_all | solution.py:83
  56.8 83.0 %all-to-all-start.1 = ((bf16[8,24,768]{2,1,0:T(8,128)(2,1)}), bf16[8,24,768]{2,1,0:T(8,128)(2,1)S(1)}, u32[]{:S(2)}, u32[]{:S(2)}) async-start(bf16[8,24,768]{2,1,0:T(8,128)(2,1)} %fusion.21), calls=%async_computation.1 | async-start | bytes 589824 | tf_op jit(solution)/shard_map/all_to_all | solution.py:89
  162.6 13.3 %all-to-all-start.2 = ((bf16[4,2,18432]{2,1,0:T(2,128)(2,1)}), bf16[4,2,18432]{2,1,0:T(2,128)(2,1)S(1)}, u32[]{:S(2)}, u32[]{:S(2)}) async-start(bf16[4,2,18432]{2,1,0:T(2,128)(2,1)} %reshape.148), calls=%async_computation.2 | async-start | bytes 589824 | tf_op jit(solution)/shard_map/all_to_all | solution.py:91
  185.7 6.8 %collective-permute-start.2 = (bf16[8,1,768]{2,1,0:T(2,128)(2,1)S(1)}, bf16[8,1,768]{2,1,0:T(2,128)(2,1)S(1)}, u32[]{:S(2)}, u32[]{:S(2)}) collective-permute-start(bf16[8,1,768]{2,1,0:T(2,128)(2,1)S(1)} %get-tuple-element.8), channel_id=1, source_target_pairs={{4,0},{8,4},{12,8},{5,1},{9,5},{13,9},{6,2},{10,6},{14,10},{7,3},{... | collective-permute-start | bytes 36872 | tf_op jit(solution)/shard_map/ppermute | solution.py:18
  189.0 6.6 %collective-permute-start.1 = (bf16[8,1,768]{2,1,0:T(2,128)(2,1)S(1)}, bf16[8,1,768]{2,1,0:T(2,128)(2,1)S(1)}, u32[]{:S(2)}, u32[]{:S(2)}) collective-permute-start(bf16[8,1,768]{2,1,0:T(2,128)(2,1)S(1)} %get-tuple-element.7), channel_id=1, source_target_pairs={{0,4},{4,8},{8,12},{1,5},{5,9},{9,13},{2,6},{6,10},{10,14},{3,7},{... | collective-permute-start | bytes 36872 | tf_op jit(solution)/shard_map/ppermute | solution.py:15
where the time goes:
time: 199 us; the launch traced here: 198 us
  other arithmetic  105 us (53%)
  local copies, waits for them, and re-layouts  34.5 us (17%)
  starting transfers between devices  21.7 us (11%)
  waiting for transfers between devices  18.8 us (9%)
  matrix products  17.8 us (9%)
    another operation x1, other arithmetic  79.5 us
    scatter-add x1, other arithmetic, local(): surface = surface.at[:, dst_idx].add(incoming)  17.6 us
    dot_general x1, matrix products, back_transform(): lax.dot_general(filtered, table_part, (((1,), (1,)), ((), ())), preferred...  9.63 us
    gather x2, local copies, waits for them, and re-layouts, local(): outgoing = jnp.transpose(surface[:, src_idx] * weights[None], (1, 0, 2))  9.47 us
    all_to_all x1, waiting for transfers between devices, local(): incr = lax.all_to_all(incr, 'gy', split_axis=2, concat_axis=0, tiled=True)  8.3 us
    dot_general x1, matrix products, circle_increment(): jnp.dot(circles.reshape(-1, cols_all), table, preferred_element_type=jnp....  8.22 us
    all_to_all x1, starting transfers between devices, local(): lax.all_to_all(crossed, ('gx', 'gy'), split_axis=0, concat_axis=0, tiled=...  7.28 us
    slice x2, local copies, waits for them, and re-layouts, local(): surface = fields[:FC].reshape(FC, cells)  6.78 us
  transfers between devices with their start and end apart: 6, of which 4 were waited for; matrix products, arithmetic and copies ran while one was open for 41% of the time, Pallas kernels for 0%

commit v1 on v0

--- a/solution.py
+++ b/solution.py
@@ -88,7 +88,9 @@
     grid_bf = fields.astype(jnp.bfloat16)
     circles = lax.all_to_all(grid_bf, "gy", split_axis=0, concat_axis=2, tiled=True)
     incr = circle_increment(circles, resp_mine, table, scale)
-    incr = lax.all_to_all(incr, "gy", split_axis=2, concat_axis=0, tiled=True)
+    incr = jnp.concatenate(
+        lax.all_to_all(jnp.stack(jnp.split(incr, lax.axis_size("gy"), axis=2)), "gy", 0, 0), axis=0
+    )
     fields = fields + incr.astype(jnp.float32)
     fields = diffuse(fields, rate) * keep[None]
     return fields[None]

time: 199 us -> 184 us (0.925)
  local copies, waits for them, and re-layouts: 34.5 us -> 24.1 us
  other arithmetic: 105 us -> 100 us
    unnamed x14, local copies, waits for them, and re-layouts: 5.79 us -> 0.03 us
    convert_element_type x1 -> x0, local copies, waits for them, and re-layouts: 2.83 us -> none  [local(): fields = fields + incr.astype(jnp.float32)]
    convert_element_type x1 -> x0, other arithmetic: 2.49 us -> none  [local(): fields = fields + incr.astype(jnp.float32)]
    another operation x1 -> x2, other arithmetic: 79.5 us -> 80.3 us
  transfers between devices with their start and end apart: 6 -> 6, of which waited for: 4 -> 4; matrix products, arithmetic and copies ran while one was open for 41% -> 43% of each run, Pallas kernels for 0% -> 0%
where the time goes in v1:
time: 184 us
  other arithmetic  100 us (54%)
  local copies, waits for them, and re-layouts  24.1 us (13%)
  starting transfers between devices  21.7 us (12%)
  waiting for transfers between devices  19.7 us (11%)
  matrix products  17.9 us (10%)
    another operation x1, other arithmetic  79.6 us
    scatter-add x1, other arithmetic, local(): surface = surface.at[:, dst_idx].add(incoming)  17.6 us
    dot_general x1, matrix products, back_transform(): lax.dot_general(filtered, table_part, (((1,), (1,)), ((), ())), preferred...  9.66 us
    gather x2, local copies, waits for them, and re-layouts, local(): outgoing = jnp.transpose(surface[:, src_idx] * weights[None], (1, 0, 2))  9.47 us
    all_to_all x1, waiting for transfers between devices, local(): lax.all_to_all(jnp.stack(jnp.split(incr, lax.axis_size('gy'), axis=2)), '...  8.3 us
    dot_general x1, matrix products, circle_increment(): jnp.dot(circles.reshape(-1, cols_all), table, preferred_element_type=jnp....  8.21 us
    all_to_all x1, starting transfers between devices, local(): lax.all_to_all(crossed, ('gx', 'gy'), split_axis=0, concat_axis=0, tiled=...  7.28 us
    slice x2, local copies, waits for them, and re-layouts, local(): surface = fields[:FC].reshape(FC, cells)  6.81 us
  transfers between devices with their start and end apart: 6, of which 4 were waited for; matrix products, arithmetic and copies ran while one was open for 43% of the time, Pallas kernels for 0%

profile of v1, /device:TPU:4, one launch (start us, length us, event | category | flops | bytes accessed | tf_op | source)
XLA Modules:
  0.0 183.6 jit_solution(3160368851103368044)
XLA Ops:
  0.0 0.0 copy-start
  0.0 0.0 copy-start.3
  0.0 0.0 copy-start.4
  0.0 0.0 copy-start.6
  0.0 0.0 copy-start.5
  0.0 1.1 fusion.28
  1.2 5.7 %copy.17 = f32[1,4,24,768]{1,3,2,0:T(8,128)} copy(f32[1,4,24,768]{3,2,1,0:T(8,128)S(1)} %get-tuple-element.5) | data formatting | bytes 589824 | tf_op jit(solution)/shard_map/slice | solution.py:80
  6.8 0.0 copy-done.3
  6.9 9.1 %gather_fusion = f32[2048,4]{1,0:T(8,128)S(1)} fusion(f32[4,18432]{0,1:T(8,128)} %bitcast.55, s32[2048]{0:T(1024)S(1)} %fusion.25), kind=kCustom, calls=%fused_computation | custom fusion | bytes 73728 | tf_op jit(solution)/shard_map/gather | solution.py:81
  16.0 0.3 copy.18
  16.3 0.0 copy-done.4
  16.3 0.0 copy-done.6
  16.3 0.1 bitcast_select_fusion
  16.4 0.1 collective-permute-start
  16.5 1.2 collective-permute-done
  17.7 0.6 copy.19
  18.3 7.3 %all-to-all-start = ((f32[16,4,128]{2,1,0:T(4,128)}), f32[16,4,128]{2,1,0:T(4,128)S(1)}, u32[]{:S(2)}, u32[]{:S(2)}) async-start(f32[16,4,128]{2,1,0:T(4,128)} %copy.19), calls=%async_computation | async-start | bytes 65536 | tf_op jit(solution)/shard_map/all_to_all | solution.py:83
  25.6 0.0 copy-done.5
  25.6 6.1 %all-to-all-done = f32[16,4,128]{2,1,0:T(4,128)S(1)} async-done(((f32[16,4,128]{2,1,0:T(4,128)}), f32[16,4,128]{2,1,0:T(4,128)S(1)}, u32[]{:S(2)}, u32[]{:S(2)}) %all-to-all-start) | async-done | bytes 32800 | tf_op jit(solution)/shard_map/all_to_all | solution.py:83
  31.7 0.4 copy.20
  32.1 17.6 %scatter_fusion = f32[4,18432]{0,1:T(8,128)} fusion(f32[4,18432]{0,1:T(8,128)} %bitcast.56, s32[2048]{0:T(1024)S(1)} %fusion.23, f32[2048,4]{1,0:T(8,128)S(1)} %copy.20), kind=kCustom, calls=%fused_computation.1 | custom fusion | flops 8192 | bytes 106496 | tf_op jit(solution)/shard_map/scatter-add | solution.py:85
  49.7 6.4 %copy.21 = f32[4,24,768]{2,1,0:T(8,128)S(1)} copy(f32[4,24,768]{0,2,1:T(8,128)} %bitcast.57) | data formatting | bytes 589824 | tf_op jit(solution)/shard_map/reshape | solution.py:86
  56.1 0.8 fusion.21
  56.8 3.5 %all-to-all-start.1 = ((bf16[8,24,768]{2,1,0:T(8,128)(2,1)}), bf16[8,24,768]{2,1,0:T(8,128)(2,1)S(1)}, u32[]{:S(2)}, u32[]{:S(2)}) async-start(bf16[8,24,768]{2,1,0:T(8,128)(2,1)} %fusion.21), calls=%async_computation.1 | async-start | bytes 589824 | tf_op jit(solution)/shard_map/all_to_all | solution.py:89
  60.3 79.6 %sine_convert_fusion = (bf16[3072,1536]{1,0:T(8,128)(2,1)}, bf16[3072,1536]{1,0:T(8,128)(2,1)}) fusion(), kind=kLoop, calls=%fused_computation.8 | loop fusion | flops 51904512 | bytes 18874368 | tf_op jit(solution)/shard_map/convert.2
  139.9 0.0 copy-done
  139.9 0.0 all-to-all-done.1
  139.9 0.2 copy.24
  140.1 0.2 dot_general.8
  140.3 8.2 %fusion.12 = bf16[2,24,3072]{2,1,0:T(8,128)(2,1)S(1)} fusion(bf16[2,24,3072]{2,1,0:T(8,128)(2,1)S(1)} %dot_general.8, bf16[3072,1536]{1,0:T(8,128)(2,1)} %get-tuple-element.13, bf16[3072,1536]{1,0:T(8,128)(2,1)} %get-tuple-element.14, f32[2,3072]{1,0:T(2,128)S(1)} %dynamic-slice_bitcast_fusion), kind=kOutput, calls=%fused_computation.17 | convolution fusion | flops 944013312 | bytes 19488768 | tf_op jit(solution)/shard_map/dot_general | solution.py:45
  148.5 0.0 copy-start.2
  148.5 0.0 copy-start.1
  148.5 9.7 %fusion.15 = bf16[48,3072]{1,0:T(8,128)(2,1)S(1)} fusion(bf16[48,3072]{1,0:T(8,128)(2,1)S(1)} %bitcast.65, bf16[3072,1536]{1,0:T(8,128)(2,1)} %get-tuple-element.13, bf16[3072,1536]{1,0:T(8,128)(2,1)} %get-tuple-element.14), kind=kOutput, calls=%fused_computation.18 | convolution fusion | flops 944013312 | bytes 19464192 | tf_op jit(solution)/shard_map/dot_general | solution.py:38
  158.2 0.8 pad_maximum_fusion.8
  159.0 5.1 %all-to-all-start.2 = ((bf16[4,2,24,768]{3,2,1,0:T(8,128)(2,1)}), bf16[4,2,24,768]{3,2,1,0:T(8,128)(2,1)S(1)}, u32[]{:S(2)}, u32[]{:S(2)}) async-start(bf16[4,2,24,768]{3,2,1,0:T(8,128)(2,1)} %pad_maximum_fusion.8), calls=%async_computation.2 | async-start | bytes 589824 | tf_op jit(solution)/shard_map/all_to_all | solution.py:92
  164.0 8.3 %all-to-all-done.2 = bf16[4,2,24,768]{3,2,1,0:T(8,128)(2,1)S(1)} async-done(((bf16[4,2,24,768]{3,2,1,0:T(8,128)(2,1)}), bf16[4,2,24,768]{3,2,1,0:T(8,128)(2,1)S(1)}, u32[]{:S(2)}, u32[]{:S(2)}) %all-to-all-start.2) | async-done | bytes 294944 | tf_op jit(solution)/shard_map/all_to_all | solution.py:92
  172.3 0.1 fusion.22
  172.5 3.4 %collective-permute-start.2 = (bf16[8,1,768]{2,1,0:T(2,128)(2,1)S(1)}, bf16[8,1,768]{2,1,0:T(2,128)(2,1)S(1)}, u32[]{:S(2)}, u32[]{:S(2)}) collective-permute-start(bf16[8,1,768]{2,1,0:T(2,128)(2,1)S(1)} %get-tuple-element.8), channel_id=1, source_target_pairs={{4,0},{8,4},{12,8},{5,1},{9,5},{13,9},{6,2},{10,6},{14,10},{7,3},{... | collective-permute-start | bytes 36872 | tf_op jit(solution)/shard_map/ppermute | solution.py:18
  175.8 2.5 %collective-permute-start.1 = (bf16[8,1,768]{2,1,0:T(2,128)(2,1)S(1)}, bf16[8,1,768]{2,1,0:T(2,128)(2,1)S(1)}, u32[]{:S(2)}, u32[]{:S(2)}) collective-permute-start(bf16[8,1,768]{2,1,0:T(2,128)(2,1)S(1)} %get-tuple-element.7), channel_id=1, source_target_pairs={{0,4},{4,8},{8,12},{1,5},{5,9},{9,13},{2,6},{6,10},{10,14},{3,7},{... | collective-permute-start | bytes 36872 | tf_op jit(solution)/shard_map/ppermute | solution.py:15
  178.3 0.0 copy-done.2
  178.3 0.0 collective-permute-done.2
  178.4 4.1 %collective-permute-done.1 = bf16[8,1,768]{2,1,0:T(2,128)(2,1)S(1)} collective-permute-done((bf16[8,1,768]{2,1,0:T(2,128)(2,1)S(1)}, bf16[8,1,768]{2,1,0:T(2,128)(2,1)S(1)}, u32[]{:S(2)}, u32[]{:S(2)}) %collective-permute-start.1) | collective-permute-done | bytes 12320 | tf_op jit(solution)/shard_map/ppermute | solution.py:15
  182.5 0.1 maximum_convert_fusion
  182.6 0.0 copy-done.1
  182.6 1.0 fusion.20
  (7 shorter events, 0.1 us)
Async XLA Ops:
  0.0 139.9 %copy-start = (f32[1,8,3072]{2,1,0:T(8,128)S(1)}, f32[1,8,3072]{2,1,0:T(8,128)}, u32[]{:S(2)}) copy-start(f32[1,8,3072]{2,1,0:T(8,128)} %param.9) | copy-start | bytes 294916
  0.0 6.8 %copy-start.3 = (s32[1,1,1,16,128]{4,3,2,1,0:T(8,128)S(1)}, s32[1,1,1,16,128]{4,3,2,1,0:T(8,128)}, u32[]{:S(2)}) copy-start(s32[1,1,1,16,128]{4,3,2,1,0:T(8,128)} %param.12) | copy-start | bytes 24580
  0.0 16.3 %copy-start.4 = (f32[1,1,1,16,128]{4,3,2,1,0:T(8,128)S(1)}, f32[1,1,1,16,128]{4,3,2,1,0:T(8,128)}, u32[]{:S(2)}) copy-start(f32[1,1,1,16,128]{4,3,2,1,0:T(8,128)} %param.14) | copy-start | bytes 24580
  0.0 16.3 %copy-start.6 = (s32[1,1,1,16]{3,2,1,0:T(1,128)S(1)}, s32[1,1,1,16]{3,2,1,0:T(1,128)}, u32[]{:S(2)}) copy-start(s32[1,1,1,16]{3,2,1,0:T(1,128)} %param.15) | copy-start | bytes 196
  0.0 25.6 %copy-start.5 = (s32[1,1,1,16,128]{4,3,2,1,0:T(8,128)S(1)}, s32[1,1,1,16,128]{4,3,2,1,0:T(8,128)}, u32[]{:S(2)}) copy-start(s32[1,1,1,16,128]{4,3,2,1,0:T(8,128)} %param.13) | copy-start | bytes 24580
  16.4 1.3 collective-permute-start
  18.3 13.4 %all-to-all-start = ((f32[16,4,128]{2,1,0:T(4,128)}), f32[16,4,128]{2,1,0:T(4,128)S(1)}, u32[]{:S(2)}, u32[]{:S(2)}) async-start(f32[16,4,128]{2,1,0:T(4,128)} %copy.19), calls=%async_computation | async-start | bytes 65536 | tf_op jit(solution)/shard_map/all_to_all | solution.py:83
  56.8 83.1 %all-to-all-start.1 = ((bf16[8,24,768]{2,1,0:T(8,128)(2,1)}), bf16[8,24,768]{2,1,0:T(8,128)(2,1)S(1)}, u32[]{:S(2)}, u32[]{:S(2)}) async-start(bf16[8,24,768]{2,1,0:T(8,128)(2,1)} %fusion.21), calls=%async_computation.1 | async-start | bytes 589824 | tf_op jit(solution)/shard_map/all_to_all | solution.py:89
  148.5 29.8 %copy-start.2 = (s32[24,768]{1,0:T(8,128)S(1)}, s32[24,768]{1,0:T(8,128)}, u32[]{:S(2)}) copy-start(s32[24,768]{1,0:T(8,128)} %param.11) | copy-start | bytes 221188
  148.5 34.1 %copy-start.1 = (f32[1,24,768]{2,1,0:T(8,128)S(1)}, f32[1,24,768]{2,1,0:T(8,128)}, u32[]{:S(2)}) copy-start(f32[1,24,768]{2,1,0:T(8,128)} %param.10) | copy-start | bytes 221188
  159.0 13.4 %all-to-all-start.2 = ((bf16[4,2,24,768]{3,2,1,0:T(8,128)(2,1)}), bf16[4,2,24,768]{3,2,1,0:T(8,128)(2,1)S(1)}, u32[]{:S(2)}, u32[]{:S(2)}) async-start(bf16[4,2,24,768]{3,2,1,0:T(8,128)(2,1)} %pad_maximum_fusion.8), calls=%async_computation.2 | async-start | bytes 589824 | tf_op jit(solution)/shard_map/all_to_all | solution.py:92
  172.5 5.9 %collective-permute-start.2 = (bf16[8,1,768]{2,1,0:T(2,128)(2,1)S(1)}, bf16[8,1,768]{2,1,0:T(2,128)(2,1)S(1)}, u32[]{:S(2)}, u32[]{:S(2)}) collective-permute-start(bf16[8,1,768]{2,1,0:T(2,128)(2,1)S(1)} %get-tuple-element.8), channel_id=1, source_target_pairs={{4,0},{8,4},{12,8},{5,1},{9,5},{13,9},{6,2},{10,6},{14,10},{7,3},{... | collective-permute-start | bytes 36872 | tf_op jit(solution)/shard_map/ppermute | solution.py:18
  175.8 6.6 %collective-permute-start.1 = (bf16[8,1,768]{2,1,0:T(2,128)(2,1)S(1)}, bf16[8,1,768]{2,1,0:T(2,128)(2,1)S(1)}, u32[]{:S(2)}, u32[]{:S(2)}) collective-permute-start(bf16[8,1,768]{2,1,0:T(2,128)(2,1)S(1)} %get-tuple-element.7), channel_id=1, source_target_pairs={{0,4},{4,8},{8,12},{1,5},{5,9},{9,13},{2,6},{6,10},{10,14},{3,7},{... | collective-permute-start | bytes 36872 | tf_op jit(solution)/shard_map/ppermute | solution.py:15
